TPU v7x, 1024 devices: a whole 8x8x8 slice. The times are simulated.
1024 devices in a mesh: gx: 64 (over x, z), gy: 16 (over y, core).
Axes of the slice: x: 8, y: 8, z: 8, core: 2. Of those that a mesh axis runs over, the one named last changes fastest.
Arguments:
- blocks: float32 [64, 16, 64, 4, 128], P('gx', 'gy'), may hold values from 0 to 1, as said below
- active_counts: int32 [64, 16], P('gx', 'gy'), may hold values from 1 to 32, as said below
- pair_lists: int32 [64, 16, 32, 16], P('gx', 'gy'), may hold values from 0 to 575
- cell_ids: int32 [64, 16, 64], P('gx', 'gy'), may hold values from 0 to 511, as said below
Outputs:
- accel: float32 [64, 16, 32, 3, 128], P('gx', 'gy')
Inputs may be any that keep to these rules, and one draw needn't show every extreme that they name: `active_counts`: every domain has at least one active block and some domain has 32; the active blocks are the first ones of the domain. `pair_lists`: entry (3 a + b) * 64 + n names block n of the domain a - 1 steps along gx and b - 1 steps along gy, with wrap around; a list may repeat a block or name the target block itself. `cell_ids`: A block of domain (i, j) lies in one of the 2 cells (g * 2 + h) with g = (i // 2) * (16 // 2) + j // 2. `blocks`: coordinates lie in [0, 1); masses are positive.
All inputs are finite; a program needn't handle non-finite values.
Results may differ from a plain program's by a relative error of at most 0.0003.
Values sent between devices are 32-bit elements; how exact they have to be, the bound alone decides.
A program may use at most 32 MiB of HBM per device.

v0:
```python
import jax
import jax.numpy as jnp
from jax import lax
from jax.experimental import pallas as pl
from jax.experimental.pallas import tpu as pltpu
from jax.sharding import PartitionSpec as P

MESH = pl.DeviceIdType.MESH
EPS2 = 0.05 * 0.05
NCH = 2
UN = 2
MX = (0, 2, 4, 6)
DN = (((1,), (1,)), ((), ()))


def split3(v):
    h = v.astype(jnp.bfloat16).astype(jnp.float32)
    r = v - h
    m = r.astype(jnp.bfloat16).astype(jnp.float32)
    return h, m, r - m


def near_kernel(lists_ref, ids_ref, blk_ref, near_ref, mx_ref, tab_ref, v_ref, p_ref, fb_ref, pb_ref, tm_ref, red_ref,
                red2_ref, row1_ref, got1_ref, row2_ref, mz_ref, hs_sem, hr_sem, s1, r1, s2, r2, s3, r3, loc_sem):
    nx, ny = 64, 16
    gx, gy = lax.axis_index("gx"), lax.axis_index("gy")
    xi, zi = gx // 8, gx % 8
    xp, xm = lax.rem(gx + 1, nx), lax.rem(gx + nx - 1, nx)
    yp, ym = lax.rem(gy + 1, ny), lax.rem(gy + ny - 1, ny)

    def ypeer(d):
        return (gx, lax.rem(gy + d, ny))

    def zpeer(d):
        return (xi * 8 + lax.rem(zi + d, 8), gy)

    def xpeer(d):
        return (lax.rem(xi + d, 8) * 8 + zi, gy)

    barrier = pltpu.get_barrier_semaphore()
    for d in range(1, ny):
        pl.semaphore_signal(barrier, inc=1, device_id=ypeer(d), device_id_type=MESH)
    for d in range(1, 8):
        pl.semaphore_signal(barrier, inc=1, device_id=zpeer(d), device_id_type=MESH)
        pl.semaphore_signal(barrier, inc=1, device_id=xpeer(d), device_id_type=MESH)
    pl.semaphore_signal(barrier, inc=1, device_id=(xp, gy), device_id_type=MESH)
    pl.semaphore_signal(barrier, inc=1, device_id=(xm, gy), device_id_type=MESH)

    own = pltpu.make_async_copy(blk_ref, tab_ref.at[pl.ds(1024, 256)], loc_sem)
    own.start()
    own.wait()

    m = tab_ref[pl.ds(1024 + 3, 64, stride=4), :]
    ids = jnp.broadcast_to(ids_ref[...] % 2, (64, 64)).astype(jnp.float32)
    eye = lax.broadcasted_iota(jnp.int32, (64, 64), 0) == lax.broadcasted_iota(jnp.int32, (64, 64), 1)
    half = jnp.sum(jnp.where(eye, ids, 0.0), axis=1, keepdims=True)
    upper = jnp.sum(jnp.sum(jnp.where(half > 0.5, m, 0.0), axis=0, keepdims=True), axis=1, keepdims=True)
    lower = jnp.sum(jnp.sum(jnp.where(half > 0.5, 0.0, m), axis=0, keepdims=True), axis=1, keepdims=True)
    lane = lax.broadcasted_iota(jnp.int32, (1, 128), 1)
    at = (gy // 2) * 2
    row = jnp.where(lane == at, lower, jnp.where(lane == at + 1, upper, 0.0))
    row1_ref[...] = row

    low = lax.broadcasted_iota(jnp.int32, (8, 128), 0) < 4
    ones = jnp.ones((8, 128), jnp.float32)

    def prepare(q):
        a, b = q // 3 - 1, q % 3 - 1
        x = tab_ref[pl.ds(q * 256, 64, stride=4), :] + (a - 0.5)
        y = tab_ref[pl.ds(q * 256 + 1, 64, stride=4), :] + (b - 0.5)
        z = tab_ref[pl.ds(q * 256 + 2, 64, stride=4), :] - 0.5
        m = tab_ref[pl.ds(q * 256 + 3, 64, stride=4), :]
        s = x * x + y * y + z * z
        for k, val in enumerate((x, y, z, s, x, y, z, s)):
            v_ref[pl.ds(q * 512 + k, 64, stride=8), :] = val
        for k, val in enumerate((m, m * x, m * y, m * z)):
            p_ref[pl.ds(q * 256 + k, 64, stride=4), :] = val

        def step(i, c):
            for u in range(4):
                j = q * 64 + i * 4 + u
                h, m, l = split3(v_ref[pl.ds(j * 8, 8), :])
                f = jnp.concatenate([jnp.where(low, h, m), jnp.where(low, l, h), jnp.where(low, m, h), ones], axis=0)
                fb_ref[j] = f.astype(jnp.bfloat16)
                h, m, l = split3(p_ref[pl.ds(j * 4, 4), :])
                pb_ref[j] = jnp.concatenate([h, m, l, l], axis=0).astype(jnp.bfloat16)
            return c

        lax.fori_loop(0, 16, step, 0)

    prepare(4)

    row8 = lax.broadcasted_iota(jnp.int32, (8, 128), 0)
    ws = (row8 & 3) == 3

    def targets(i, c):
        for u in range(4):
            t = i * 4 + u
            v = v_ref[pl.ds((256 + t) * 8, 8), :]
            h, m, l = split3(-2.0 * v)
            h = jnp.where(ws, 1.0, h)
            m = jnp.where(ws, 0.0, m)
            l = jnp.where(ws, 0.0, l)
            qh, qm, ql = split3(v[3:4, :] + EPS2)
            qg = jnp.where(row8 == 0, qh, jnp.where(row8 == 1, qm, jnp.where(row8 == 2, ql, 0.0)))
            tt = jnp.concatenate([h, jnp.where(low, h, m), jnp.where(low, m, l), qg], axis=0)
            tm_ref[t] = jnp.transpose(tt).astype(jnp.bfloat16)
        return c

    lax.fori_loop(0, 8, targets, 0)
    red_ref[0:UN] = jnp.zeros((UN, 128, 128), jnp.float32)
    red2_ref[0:UN] = jnp.zeros((UN, 128, 16), jnp.float32)

    pl.semaphore_wait(barrier, 31)

    phase1 = [
        pltpu.make_async_remote_copy(row1_ref, got1_ref.at[d - 1], s1.at[d - 1], r1.at[d - 1],
                                     device_id=ypeer(d), device_id_type=MESH)
        for d in range(1, ny)
    ]
    for c in phase1:
        c.start()

    size = 256 // NCH

    def halo(index, ch, source, slot, device):
        src = blk_ref.at[pl.ds(ch * size, size)] if source is None else tab_ref.at[pl.ds(source * 256 + ch * size, size)]
        k = index * NCH + ch
        return pltpu.make_async_remote_copy(src, tab_ref.at[pl.ds(slot * 256 + ch * size, size)], hs_sem.at[k],
                                            hr_sem.at[k], device_id=device, device_id_type=MESH)

    toxp = [halo(0, ch, None, 1, (xp, gy)) for ch in range(NCH)]
    toxm = [halo(1, ch, None, 7, (xm, gy)) for ch in range(NCH)]
    toyp = [halo(2, ch, None, 3, (gx, yp)) for ch in range(NCH)]
    toym = [halo(3, ch, None, 5, (gx, ym)) for ch in range(NCH)]
    fwd = {4: [], 5: [], 6: [], 7: []}
    for ch in range(NCH):
        for c in (toxp, toxm, toyp, toym):
            c[ch].start()

    def forward(ch):
        for index, arrived, source, slot, device in ((4, toxp, 1, 0, (gx, yp)), (6, None, 1, 2, (gx, ym)),
                                                     (5, toxm, 7, 6, (gx, yp)), (7, None, 7, 8, (gx, ym))):
            if arrived is not None:
                arrived[ch].wait_recv()
            c = halo(index, ch, source, slot, device)
            c.start()
            fwd[index].append(c)

    forward(0)
    for c in phase1:
        c.wait_recv()
    total = row
    for d in range(1, ny):
        total = total + got1_ref[d - 1]
    row2_ref[...] = total
    mz_ref[zi] = total
    for ch in range(1, NCH):
        forward(ch)
    phase2 = [
        pltpu.make_async_remote_copy(row2_ref, mz_ref.at[zi], s2.at[d - 1], r2.at[d - 1],
                                     device_id=zpeer(d), device_id_type=MESH)
        for d in range(1, 8)
    ]
    for c in phase2:
        c.start()
    prepare(1)
    prepare(7)
    for c in toyp:
        c.wait_recv()
    prepare(3)
    for c in toym:
        c.wait_recv()
    prepare(5)
    for index, slot in ((4, 0), (6, 2), (5, 6), (7, 8)):
        for c in fwd[index]:
            c.wait_recv()
        prepare(slot)
    for c in phase2:
        c.wait_recv()
    phase3 = [
        pltpu.make_async_remote_copy(mz_ref, mx_ref.at[xi], s3.at[d - 1], r3.at[d - 1],
                                     device_id=xpeer(d), device_id_type=MESH)
        for d in range(1, 8)
    ]
    for c in phase3:
        c.start()
    mx_ref[xi] = mz_ref[...]

    lane128 = lax.broadcasted_iota(jnp.int32, (128, 128), 1)

    def pairs(t):
        tm = tm_ref[t]
        accs, acc2 = None, None
        for k in range(8):
            i0, i1 = lists_ref[2 * k, t], lists_ref[2 * k + 1, t]
            f = jnp.concatenate([fb_ref[i0], fb_ref[i1]], axis=1)
            d = jnp.dot(tm, f, preferred_element_type=jnp.float32)
            r = lax.rsqrt(d)
            w = r * r * r
            if k in MX:
                p = jnp.concatenate([pb_ref[i0], pb_ref[i1]], axis=1)
                hi = w.astype(jnp.bfloat16)
                lo = (w - hi.astype(jnp.float32)).astype(jnp.bfloat16)
                y = lax.dot_general(hi, p, DN, preferred_element_type=jnp.float32)
                acc2 = y if acc2 is None else acc2 + y
                acc2 = acc2 + lax.dot_general(lo, p, DN, preferred_element_type=jnp.float32)
                continue
            for u, ii in enumerate((i0, i1)):
                wu = w[:, u * 128:(u + 1) * 128]
                g = [p_ref[pl.ds(ii * 4 + cc, 1), :] * wu for cc in range(4)]
                accs = g if accs is None else [x + y for x, y in zip(accs, g)]
        red2_ref[t] = acc2
        rr = [jnp.sum(x, axis=1, keepdims=True) for x in accs]
        red_ref[t] = jnp.where(lane128 == 0, rr[0], jnp.where(lane128 == 1, rr[1], jnp.where(lane128 == 2, rr[2], rr[3])))

    def reduce(t):
        v = v_ref[pl.ds((256 + t) * 8, 8), :]
        r2 = jnp.transpose(red2_ref[t])
        red = jnp.transpose(red_ref[t])[0:4] + (r2[0:4] + r2[4:8] + r2[8:12])
        for c in range(3):
            near_ref[c, pl.ds(t, 1), :] = red[c + 1:c + 2] - v[c:c + 1, :] * red[0:1]

    def slots(i, c):
        for u in range(UN):
            pairs(i * UN + u)
        for u in range(UN):
            reduce(jnp.maximum(i - 1, 0) * UN + u)
        return c

    lax.fori_loop(0, 32 // UN, slots, 0)
    for u in range(UN):
        reduce(32 - UN + u)

    for c in phase3:
        c.wait_recv()
    for c in phase1 + phase2 + phase3 + toxp + toxm + toyp + toym + fwd[4] + fwd[5] + fwd[6] + fwd[7]:
        c.wait_send()


def near(lists, ids, blk):
    dma = pltpu.SemaphoreType.DMA
    return pl.pallas_call(
        near_kernel,
        out_shape=(jax.ShapeDtypeStruct((3, 32, 128), jnp.float32), jax.ShapeDtypeStruct((8, 8, 1, 128), jnp.float32)),
        in_specs=[pl.BlockSpec(memory_space=pltpu.SMEM), pl.BlockSpec(memory_space=pltpu.VMEM),
                  pl.BlockSpec(memory_space=pl.ANY)],
        out_specs=(pl.BlockSpec(memory_space=pltpu.VMEM), pl.BlockSpec(memory_space=pltpu.VMEM)),
        scratch_shapes=[
            pltpu.VMEM((2304, 128), jnp.float32), pltpu.VMEM((4608, 128), jnp.float32),
            pltpu.VMEM((2304, 128), jnp.float32), pltpu.VMEM((576, 32, 128), jnp.bfloat16),
            pltpu.VMEM((576, 16, 128), jnp.bfloat16), pltpu.VMEM((32, 128, 32), jnp.bfloat16),
            pltpu.VMEM((32, 128, 128), jnp.float32), pltpu.VMEM((32, 128, 16), jnp.float32),
            pltpu.VMEM((1, 128), jnp.float32), pltpu.VMEM((15, 1, 128), jnp.float32),
            pltpu.VMEM((1, 128), jnp.float32), pltpu.VMEM((8, 1, 128), jnp.float32),
            dma((8 * NCH,)), dma((8 * NCH,)), dma((15,)), dma((15,)), dma((7,)), dma((7,)), dma((7,)), dma((7,)), dma,
        ],
        compiler_params=pltpu.CompilerParams(collective_id=0, has_side_effects=True),
        name="near",
    )(lists, ids, blk)


def far_kernel(count_ref, blk_ref, mass_ref, near_ref, out_ref, mb_ref):
    gx = lax.axis_index("gx").astype(jnp.float32)
    gy = lax.axis_index("gy").astype(jnp.float32)
    mt = jnp.transpose(mass_ref[...])[:16, :]
    for g in range(32):
        mb_ref[pl.ds(g * 16, 16), :] = jnp.broadcast_to(mt[:, 2 * g:2 * g + 1] + mt[:, 2 * g + 1:2 * g + 2], (16, 128))
    row8 = lax.broadcasted_iota(jnp.int32, (8, 128), 0)

    def group(s, c):
        x = blk_ref[pl.ds(s * 32, 8, stride=4), :]
        y = blk_ref[pl.ds(s * 32 + 1, 8, stride=4), :]
        z = blk_ref[pl.ds(s * 32 + 2, 8, stride=4), :]
        dz = [0.25 - z, 0.75 - z]
        dy = [(2.0 * j + 1.0 - gy) - y for j in range(8)]
        zz = [d * d + 1.0 for d in dz]
        yy = [d * d for d in dy]
        base = [[yy[j] + zz[h] for h in range(2)] for j in range(8)]
        by, bz, ax = [None] * 8, [None] * 2, None
        for g in range(32):
            dx = (2.0 * g + 1.0 - gx) - x
            xx = dx * dx
            total = None
            for j in range(8):
                w = []
                for h in range(2):
                    r = lax.rsqrt(base[j][h] + xx)
                    v = (r * r) * (r * mb_ref[pl.ds(g * 16 + j * 2 + h, 1), :])
                    w.append(v)
                bz[1] = w[1] if bz[1] is None else bz[1] + w[1]
                bz[0] = w[0] if bz[0] is None else bz[0] + w[0]
                both = w[0] + w[1]
                by[j] = both if by[j] is None else by[j] + both
                total = both if total is None else total + both
            ax = total * dx if ax is None else ax + total * dx
        ay = by[0] * dy[0]
        for j in range(1, 8):
            ay = ay + by[j] * dy[j]
        az = bz[0] * dz[0] + bz[1] * dz[1]
        active = row8 + s * 8 < count_ref[0, 0]
        for k, val in enumerate((ax, ay, az)):
            at = pl.ds(pl.multiple_of(s * 8, 8), 8)
            out_ref[k, at, :] = jnp.where(active, near_ref[k, at, :] + val, 0.0)
        return c

    lax.fori_loop(0, 4, group, 0)


def far(count, blk, mass, near_part):
    return pl.pallas_call(
        far_kernel,
        out_shape=jax.ShapeDtypeStruct((3, 32, 128), jnp.float32),
        in_specs=[pl.BlockSpec(memory_space=pltpu.SMEM)] + [pl.BlockSpec(memory_space=pltpu.VMEM)] * 3,
        out_specs=pl.BlockSpec(memory_space=pltpu.VMEM),
        scratch_shapes=[pltpu.VMEM((512, 128), jnp.float32)],
        name="far",
    )(count, blk, mass, near_part)


def body(blocks, active_counts, pair_lists, cell_ids):
    blk = blocks.reshape(256, 128)
    near_part, mass = near(pair_lists[0, 0].T, cell_ids[0], blk)
    out = far(active_counts, blk, mass.reshape(64, 128), near_part)
    return out.transpose(1, 0, 2)[None, None]


def solution(mesh):
    in_specs = (P("gx", "gy", None, None, None), P("gx", "gy"), P("gx", "gy", None, None), P("gx", "gy", None))
    return jax.shard_map(body, mesh=mesh, in_specs=in_specs, out_specs=P("gx", "gy", None, None, None),
                         check_vma=False)
```

profile of v0, /device:TPU:1, one launch (start us, length us, event | category | flops | bytes accessed | tf_op | source)
XLA Modules:
  0.0 57.1 jit_solution(9369008362941642264)
XLA Ops:
  0.7 52.4 %near.1 = (f32[3,32,128]{2,1,0:T(8,128)}, f32[8,8,1,128]{3,2,1,0:T(1,128)}) custom-call(s32[16,32]{1,0:T(8,128)} %bitcast.12, s32[1,64]{1,0:T(1,128)} %bitcast.13, f32[256,128]{1,0:T(8,128)} %bitcast.9), custom_call_target="tpu_custom_call" | custom-call | tf_op jit(solution)/shard_map/near/pallas_call | solution.py:243
  53.0 4.1 %far.1 = f32[3,32,128]{2,1,0:T(8,128)} custom-call(s32[1,1]{1,0:T(1,128)S(6)} %copy.5.count_ref, f32[256,128]{1,0:T(8,128)} %bitcast.10, f32[64,128]{1,0:T(8,128)} %bitcast.11, f32[3,32,128]{2,1,0:T(8,128)} %get-tuple-element.8.near_ref), custom_call_target="tpu_custom_call" | custom-call | tf_op jit(solution)/shard_map/far/pallas_call | solution.py:311
where the time goes:
time: 57.4 us; the launch traced here: 57.1 us
  Pallas kernels  56.5 us (98%)
  between operations  0.66 us (1%)
    pallas_call x1, Pallas kernels, near(): pl.pallas_call(near_kernel, out_shape=(jax.ShapeDtypeStruct((3, 32, 128),...  52.4 us
    pallas_call x1, Pallas kernels, far(): pl.pallas_call(far_kernel, out_shape=jax.ShapeDtypeStruct((3, 32, 128), j...  4.12 us

commit v1 on v0

--- a/solution.py
+++ b/solution.py
@@ -7,8 +7,8 @@
 
 MESH = pl.DeviceIdType.MESH
 EPS2 = 0.05 * 0.05
-NCH = 2
-UN = 2
+NCH = 4
+UN = 4
 MX = (0, 2, 4, 6)
 DN = (((1,), (1,)), ((), ()))
 
@@ -20,7 +20,7 @@
     return h, m, r - m
 
 
-def near_kernel(lists_ref, ids_ref, blk_ref, near_ref, mx_ref, tab_ref, v_ref, p_ref, fb_ref, pb_ref, tm_ref, red_ref,
+def force_kernel(lists_ref, count_ref, ids_ref, blk_ref, out_ref, mx_ref, near_ref, q_ref, mb_ref, tab_ref, v_ref, p_ref, fb_ref, pb_ref, tm_ref, red_ref,
                 red2_ref, row1_ref, got1_ref, row2_ref, mz_ref, hs_sem, hr_sem, s1, r1, s2, r2, s3, r3, loc_sem):
     nx, ny = 64, 16
     gx, gy = lax.axis_index("gx"), lax.axis_index("gy")
@@ -48,6 +48,26 @@
 
     own = pltpu.make_async_copy(blk_ref, tab_ref.at[pl.ds(1024, 256)], loc_sem)
     own.start()
+
+    pl.semaphore_wait(barrier, 31)
+
+    size = 256 // NCH
+
+    def halo(index, ch, source, slot, device):
+        src = blk_ref.at[pl.ds(ch * size, size)] if source is None else tab_ref.at[pl.ds(source * 256 + ch * size, size)]
+        k = index * NCH + ch
+        return pltpu.make_async_remote_copy(src, tab_ref.at[pl.ds(slot * 256 + ch * size, size)], hs_sem.at[k],
+                                            hr_sem.at[k], device_id=device, device_id_type=MESH)
+
+    toxp = [halo(0, ch, None, 1, (xp, gy)) for ch in range(NCH)]
+    toxm = [halo(1, ch, None, 7, (xm, gy)) for ch in range(NCH)]
+    toyp = [halo(2, ch, None, 3, (gx, yp)) for ch in range(NCH)]
+    toym = [halo(3, ch, None, 5, (gx, ym)) for ch in range(NCH)]
+    fwd = {4: [], 5: [], 6: [], 7: []}
+    for ch in range(NCH):
+        for c in (toxp, toxm, toyp, toym):
+            c[ch].start()
+
     own.wait()
 
     m = tab_ref[pl.ds(1024 + 3, 64, stride=4), :]
@@ -61,6 +81,14 @@
     row = jnp.where(lane == at, lower, jnp.where(lane == at + 1, upper, 0.0))
     row1_ref[...] = row
 
+    phase1 = [
+        pltpu.make_async_remote_copy(row1_ref, got1_ref.at[d - 1], s1.at[d - 1], r1.at[d - 1],
+                                     device_id=ypeer(d), device_id_type=MESH)
+        for d in range(1, ny)
+    ]
+    for c in phase1:
+        c.start()
+
     low = lax.broadcasted_iota(jnp.int32, (8, 128), 0) < 4
     ones = jnp.ones((8, 128), jnp.float32)
 
@@ -73,8 +101,8 @@
         s = x * x + y * y + z * z
         for k, val in enumerate((x, y, z, s, x, y, z, s)):
             v_ref[pl.ds(q * 512 + k, 64, stride=8), :] = val
-        for k, val in enumerate((m, m * x, m * y, m * z)):
-            p_ref[pl.ds(q * 256 + k, 64, stride=4), :] = val
+        for k, val in enumerate((m, m * x, m * y, m * z) * 2):
+            p_ref[pl.ds(q * 512 + k, 64, stride=8), :] = val
 
         def step(i, c):
             for u in range(4):
@@ -82,13 +110,11 @@
                 h, m, l = split3(v_ref[pl.ds(j * 8, 8), :])
                 f = jnp.concatenate([jnp.where(low, h, m), jnp.where(low, l, h), jnp.where(low, m, h), ones], axis=0)
                 fb_ref[j] = f.astype(jnp.bfloat16)
-                h, m, l = split3(p_ref[pl.ds(j * 4, 4), :])
-                pb_ref[j] = jnp.concatenate([h, m, l, l], axis=0).astype(jnp.bfloat16)
+                h, m, l = split3(p_ref[pl.ds(j * 8, 8), :])
+                pb_ref[j] = jnp.concatenate([jnp.where(low, h, m), l], axis=0).astype(jnp.bfloat16)
             return c
 
         lax.fori_loop(0, 16, step, 0)
-
-    prepare(4)
 
     row8 = lax.broadcasted_iota(jnp.int32, (8, 128), 0)
     ws = (row8 & 3) == 3
@@ -107,37 +133,6 @@
             tm_ref[t] = jnp.transpose(tt).astype(jnp.bfloat16)
         return c
 
-    lax.fori_loop(0, 8, targets, 0)
-    red_ref[0:UN] = jnp.zeros((UN, 128, 128), jnp.float32)
-    red2_ref[0:UN] = jnp.zeros((UN, 128, 16), jnp.float32)
-
-    pl.semaphore_wait(barrier, 31)
-
-    phase1 = [
-        pltpu.make_async_remote_copy(row1_ref, got1_ref.at[d - 1], s1.at[d - 1], r1.at[d - 1],
-                                     device_id=ypeer(d), device_id_type=MESH)
-        for d in range(1, ny)
-    ]
-    for c in phase1:
-        c.start()
-
-    size = 256 // NCH
-
-    def halo(index, ch, source, slot, device):
-        src = blk_ref.at[pl.ds(ch * size, size)] if source is None else tab_ref.at[pl.ds(source * 256 + ch * size, size)]
-        k = index * NCH + ch
-        return pltpu.make_async_remote_copy(src, tab_ref.at[pl.ds(slot * 256 + ch * size, size)], hs_sem.at[k],
-                                            hr_sem.at[k], device_id=device, device_id_type=MESH)
-
-    toxp = [halo(0, ch, None, 1, (xp, gy)) for ch in range(NCH)]
-    toxm = [halo(1, ch, None, 7, (xm, gy)) for ch in range(NCH)]
-    toyp = [halo(2, ch, None, 3, (gx, yp)) for ch in range(NCH)]
-    toym = [halo(3, ch, None, 5, (gx, ym)) for ch in range(NCH)]
-    fwd = {4: [], 5: [], 6: [], 7: []}
-    for ch in range(NCH):
-        for c in (toxp, toxm, toyp, toym):
-            c[ch].start()
-
     def forward(ch):
         for index, arrived, source, slot, device in ((4, toxp, 1, 0, (gx, yp)), (6, None, 1, 2, (gx, ym)),
                                                      (5, toxm, 7, 6, (gx, yp)), (7, None, 7, 8, (gx, ym))):
@@ -147,7 +142,39 @@
             c.start()
             fwd[index].append(c)
 
-    forward(0)
+    fgx, fgy = gx.astype(jnp.float32), gy.astype(jnp.float32)
+
+    def offsets(s):
+        x = tab_ref[pl.ds(1024 + s * 32, 8, stride=4), :]
+        y = tab_ref[pl.ds(1024 + s * 32 + 1, 8, stride=4), :]
+        z = tab_ref[pl.ds(1024 + s * 32 + 2, 8, stride=4), :]
+        return x, [(2.0 * j + 1.0 - fgy) - y for j in range(8)], [0.25 - z, 0.75 - z]
+
+    def weights(s):
+        x, dy, dz = offsets(s)
+        zz = [d * d + 1.0 for d in dz]
+        yy = [d * d for d in dy]
+        base = [yy[j] + zz[h] for j in range(8) for h in range(2)]
+
+        def step(i, c):
+            for u in range(4):
+                g = i * 4 + u
+                dx = (2.0 * g.astype(jnp.float32) + 1.0 - fgx) - x
+                xx = dx * dx
+                for k in range(16):
+                    r = lax.rsqrt(base[k] + xx)
+                    q_ref[s, g * 16 + k] = r * r * r
+            return c
+
+        lax.fori_loop(0, 8, step, 0)
+
+    prepare(4)
+    for ch in range(NCH):
+        forward(ch)
+        weights(ch)
+    lax.fori_loop(0, 8, targets, 0)
+    red_ref[0:UN] = jnp.zeros((UN, 128, 128), jnp.float32)
+    red2_ref[0:UN] = jnp.zeros((UN, 128, 16), jnp.float32)
     for c in phase1:
         c.wait_recv()
     total = row
@@ -155,8 +182,6 @@
         total = total + got1_ref[d - 1]
     row2_ref[...] = total
     mz_ref[zi] = total
-    for ch in range(1, NCH):
-        forward(ch)
     phase2 = [
         pltpu.make_async_remote_copy(row2_ref, mz_ref.at[zi], s2.at[d - 1], r2.at[d - 1],
                                      device_id=zpeer(d), device_id_type=MESH)
@@ -208,7 +233,7 @@
                 continue
             for u, ii in enumerate((i0, i1)):
                 wu = w[:, u * 128:(u + 1) * 128]
-                g = [p_ref[pl.ds(ii * 4 + cc, 1), :] * wu for cc in range(4)]
+                g = [p_ref[pl.ds(ii * 8 + cc, 1), :] * wu for cc in range(4)]
                 accs = g if accs is None else [x + y for x, y in zip(accs, g)]
         red2_ref[t] = acc2
         rr = [jnp.sum(x, axis=1, keepdims=True) for x in accs]
@@ -234,62 +259,19 @@
 
     for c in phase3:
         c.wait_recv()
-    for c in phase1 + phase2 + phase3 + toxp + toxm + toyp + toym + fwd[4] + fwd[5] + fwd[6] + fwd[7]:
-        c.wait_send()
-
-
-def near(lists, ids, blk):
-    dma = pltpu.SemaphoreType.DMA
-    return pl.pallas_call(
-        near_kernel,
-        out_shape=(jax.ShapeDtypeStruct((3, 32, 128), jnp.float32), jax.ShapeDtypeStruct((8, 8, 1, 128), jnp.float32)),
-        in_specs=[pl.BlockSpec(memory_space=pltpu.SMEM), pl.BlockSpec(memory_space=pltpu.VMEM),
-                  pl.BlockSpec(memory_space=pl.ANY)],
-        out_specs=(pl.BlockSpec(memory_space=pltpu.VMEM), pl.BlockSpec(memory_space=pltpu.VMEM)),
-        scratch_shapes=[
-            pltpu.VMEM((2304, 128), jnp.float32), pltpu.VMEM((4608, 128), jnp.float32),
-            pltpu.VMEM((2304, 128), jnp.float32), pltpu.VMEM((576, 32, 128), jnp.bfloat16),
-            pltpu.VMEM((576, 16, 128), jnp.bfloat16), pltpu.VMEM((32, 128, 32), jnp.bfloat16),
-            pltpu.VMEM((32, 128, 128), jnp.float32), pltpu.VMEM((32, 128, 16), jnp.float32),
-            pltpu.VMEM((1, 128), jnp.float32), pltpu.VMEM((15, 1, 128), jnp.float32),
-            pltpu.VMEM((1, 128), jnp.float32), pltpu.VMEM((8, 1, 128), jnp.float32),
-            dma((8 * NCH,)), dma((8 * NCH,)), dma((15,)), dma((15,)), dma((7,)), dma((7,)), dma((7,)), dma((7,)), dma,
-        ],
-        compiler_params=pltpu.CompilerParams(collective_id=0, has_side_effects=True),
-        name="near",
-    )(lists, ids, blk)
-
-
-def far_kernel(count_ref, blk_ref, mass_ref, near_ref, out_ref, mb_ref):
-    gx = lax.axis_index("gx").astype(jnp.float32)
-    gy = lax.axis_index("gy").astype(jnp.float32)
-    mt = jnp.transpose(mass_ref[...])[:16, :]
+    mt = jnp.transpose(mx_ref[...].reshape(64, 128))[:16, :]
     for g in range(32):
         mb_ref[pl.ds(g * 16, 16), :] = jnp.broadcast_to(mt[:, 2 * g:2 * g + 1] + mt[:, 2 * g + 1:2 * g + 2], (16, 128))
-    row8 = lax.broadcasted_iota(jnp.int32, (8, 128), 0)
-
-    def group(s, c):
-        x = blk_ref[pl.ds(s * 32, 8, stride=4), :]
-        y = blk_ref[pl.ds(s * 32 + 1, 8, stride=4), :]
-        z = blk_ref[pl.ds(s * 32 + 2, 8, stride=4), :]
-        dz = [0.25 - z, 0.75 - z]
-        dy = [(2.0 * j + 1.0 - gy) - y for j in range(8)]
-        zz = [d * d + 1.0 for d in dz]
-        yy = [d * d for d in dy]
-        base = [[yy[j] + zz[h] for h in range(2)] for j in range(8)]
+
+    def far(s, c):
+        x, dy, dz = offsets(s)
         by, bz, ax = [None] * 8, [None] * 2, None
         for g in range(32):
-            dx = (2.0 * g + 1.0 - gx) - x
-            xx = dx * dx
+            dx = (2.0 * g + 1.0 - fgx) - x
             total = None
             for j in range(8):
-                w = []
-                for h in range(2):
-                    r = lax.rsqrt(base[j][h] + xx)
-                    v = (r * r) * (r * mb_ref[pl.ds(g * 16 + j * 2 + h, 1), :])
-                    w.append(v)
-                bz[1] = w[1] if bz[1] is None else bz[1] + w[1]
-                bz[0] = w[0] if bz[0] is None else bz[0] + w[0]
+                w = [q_ref[s, g * 16 + j * 2 + h] * mb_ref[pl.ds(g * 16 + j * 2 + h, 1), :] for h in range(2)]
+                bz = [w[h] if bz[h] is None else bz[h] + w[h] for h in range(2)]
                 both = w[0] + w[1]
                 by[j] = both if by[j] is None else by[j] + both
                 total = both if total is None else total + both
@@ -304,24 +286,37 @@
             out_ref[k, at, :] = jnp.where(active, near_ref[k, at, :] + val, 0.0)
         return c
 
-    lax.fori_loop(0, 4, group, 0)
-
-
-def far(count, blk, mass, near_part):
+    lax.fori_loop(0, 4, far, 0)
+    for c in phase1 + phase2 + phase3 + toxp + toxm + toyp + toym + fwd[4] + fwd[5] + fwd[6] + fwd[7]:
+        c.wait_send()
+
+
+def forces(lists, count, ids, blk):
+    dma = pltpu.SemaphoreType.DMA
     return pl.pallas_call(
-        far_kernel,
+        force_kernel,
         out_shape=jax.ShapeDtypeStruct((3, 32, 128), jnp.float32),
-        in_specs=[pl.BlockSpec(memory_space=pltpu.SMEM)] + [pl.BlockSpec(memory_space=pltpu.VMEM)] * 3,
+        in_specs=[pl.BlockSpec(memory_space=pltpu.SMEM)] * 2 + [pl.BlockSpec(memory_space=pltpu.VMEM),
+                  pl.BlockSpec(memory_space=pl.ANY)],
         out_specs=pl.BlockSpec(memory_space=pltpu.VMEM),
-        scratch_shapes=[pltpu.VMEM((512, 128), jnp.float32)],
-        name="far",
-    )(count, blk, mass, near_part)
+        scratch_shapes=[
+            pltpu.VMEM((8, 8, 1, 128), jnp.float32), pltpu.VMEM((3, 32, 128), jnp.float32),
+            pltpu.VMEM((4, 512, 8, 128), jnp.float32), pltpu.VMEM((512, 128), jnp.float32),
+            pltpu.VMEM((2304, 128), jnp.float32), pltpu.VMEM((4608, 128), jnp.float32),
+            pltpu.VMEM((4608, 128), jnp.float32), pltpu.VMEM((576, 32, 128), jnp.bfloat16),
+            pltpu.VMEM((576, 16, 128), jnp.bfloat16), pltpu.VMEM((32, 128, 32), jnp.bfloat16),
+            pltpu.VMEM((32, 128, 128), jnp.float32), pltpu.VMEM((32, 128, 16), jnp.float32),
+            pltpu.VMEM((1, 128), jnp.float32), pltpu.VMEM((15, 1, 128), jnp.float32),
+            pltpu.VMEM((1, 128), jnp.float32), pltpu.VMEM((8, 1, 128), jnp.float32),
+            dma((8 * NCH,)), dma((8 * NCH,)), dma((15,)), dma((15,)), dma((7,)), dma((7,)), dma((7,)), dma((7,)), dma,
+        ],
+        compiler_params=pltpu.CompilerParams(collective_id=0, has_side_effects=True),
+        name="forces",
+    )(lists, count, ids, blk)
 
 
 def body(blocks, active_counts, pair_lists, cell_ids):
-    blk = blocks.reshape(256, 128)
-    near_part, mass = near(pair_lists[0, 0].T, cell_ids[0], blk)
-    out = far(active_counts, blk, mass.reshape(64, 128), near_part)
+    out = forces(pair_lists[0, 0].T, active_counts, cell_ids[0], blocks.reshape(256, 128))
     return out.transpose(1, 0, 2)[None, None]
 
 

time: 57.4 us -> 54.6 us (0.951)
  Pallas kernels: 56.5 us -> 52.2 us
  local copies, waits for them, and re-layouts: 0 us -> 1.42 us
    pallas_call x2 -> x1, Pallas kernels: 56.5 us -> 52.2 us  [forces(): pl.pallas_call(force_kernel, out_shape=jax.ShapeDtypeStruct((3, 32, 128),...]
    unnamed x0 -> x1, local copies, waits for them, and re-layouts: none -> 1.42 us
where the time goes in v1:
time: 54.6 us; the launch traced here: 54.3 us
  Pallas kernels  52.2 us (96%)
  local copies, waits for them, and re-layouts  1.42 us (3%)
  between operations  0.66 us (1%)
    pallas_call x1, Pallas kernels, forces(): pl.pallas_call(force_kernel, out_shape=jax.ShapeDtypeStruct((3, 32, 128),...  52.2 us
    unnamed x1, local copies, waits for them, and re-layouts  1.42 us

profile of v1, /device:TPU:1, one launch (start us, length us, event | category | flops | bytes accessed | tf_op | source)
XLA Modules:
  0.0 54.3 jit_solution(14195644283669920230)
XLA Ops:
  0.7 52.2 %forces.1 = f32[3,32,128]{2,1,0:T(8,128)} custom-call(s32[16,32]{1,0:T(8,128)} %bitcast.10, s32[1,1]{1,0:T(1,128)S(6)} %copy.6.count_ref, s32[1,64]{1,0:T(1,128)} %bitcast.11, f32[256,128]{1,0:T(8,128)} %bitcast.9), custom_call_target="tpu_custom_call" | custom-call | tf_op jit(solution)/shard_map/forces/pallas_call | solution.py:296
  52.9 1.4 %copy.7 = f32[1,1,32,3,128]{4,2,3,1,0:T(8,128)} copy(f32[1,1,32,3,128]{4,2,3,1,0:T(8,128)} %bitcast.8) | data formatting | bytes 98304

commit v2 on v1

--- a/solution.py
+++ b/solution.py
@@ -34,22 +34,23 @@
     def zpeer(d):
         return (xi * 8 + lax.rem(zi + d, 8), gy)
 
-    def xpeer(d):
-        return (lax.rem(xi + d, 8) * 8 + zi, gy)
+    def xpeer(b):
+        return ((xi + b - 2 * b * ((xi // b) % 2)) * 8 + zi, gy)
 
     barrier = pltpu.get_barrier_semaphore()
     for d in range(1, ny):
         pl.semaphore_signal(barrier, inc=1, device_id=ypeer(d), device_id_type=MESH)
     for d in range(1, 8):
         pl.semaphore_signal(barrier, inc=1, device_id=zpeer(d), device_id_type=MESH)
-        pl.semaphore_signal(barrier, inc=1, device_id=xpeer(d), device_id_type=MESH)
+    for b in (1, 2, 4):
+        pl.semaphore_signal(barrier, inc=1, device_id=xpeer(b), device_id_type=MESH)
     pl.semaphore_signal(barrier, inc=1, device_id=(xp, gy), device_id_type=MESH)
     pl.semaphore_signal(barrier, inc=1, device_id=(xm, gy), device_id_type=MESH)
 
     own = pltpu.make_async_copy(blk_ref, tab_ref.at[pl.ds(1024, 256)], loc_sem)
     own.start()
 
-    pl.semaphore_wait(barrier, 31)
+    pl.semaphore_wait(barrier, 27)
 
     size = 256 // NCH
 
@@ -203,14 +204,17 @@
         prepare(slot)
     for c in phase2:
         c.wait_recv()
-    phase3 = [
-        pltpu.make_async_remote_copy(mz_ref, mx_ref.at[xi], s3.at[d - 1], r3.at[d - 1],
-                                     device_id=xpeer(d), device_id_type=MESH)
-        for d in range(1, 8)
-    ]
-    for c in phase3:
-        c.start()
     mx_ref[xi] = mz_ref[...]
+
+    def double(k):
+        b = 1 << k
+        part = mx_ref.at[pl.ds((xi // b) * b, b)]
+        return pltpu.make_async_remote_copy(part, part, s3.at[k], r3.at[k], device_id=xpeer(b), device_id_type=MESH)
+
+    first = pltpu.make_async_remote_copy(mz_ref, mx_ref.at[xi], s3.at[0], r3.at[0], device_id=xpeer(1),
+                                         device_id_type=MESH)
+    phase3 = [first, double(1), double(2)]
+    phase3[0].start()
 
     lane128 = lax.broadcasted_iota(jnp.int32, (128, 128), 1)
 
@@ -253,12 +257,16 @@
             reduce(jnp.maximum(i - 1, 0) * UN + u)
         return c
 
-    lax.fori_loop(0, 32 // UN, slots, 0)
+    steps = 32 // UN
+    cuts = (0, steps // 4, 5 * steps // 8, steps)
+    for k in range(3):
+        lax.fori_loop(cuts[k], cuts[k + 1], slots, 0)
+        phase3[k].wait_recv()
+        if k < 2:
+            phase3[k + 1].start()
     for u in range(UN):
         reduce(32 - UN + u)
 
-    for c in phase3:
-        c.wait_recv()
     mt = jnp.transpose(mx_ref[...].reshape(64, 128))[:16, :]
     for g in range(32):
         mb_ref[pl.ds(g * 16, 16), :] = jnp.broadcast_to(mt[:, 2 * g:2 * g + 1] + mt[:, 2 * g + 1:2 * g + 2], (16, 128))
@@ -308,7 +316,7 @@
             pltpu.VMEM((32, 128, 128), jnp.float32), pltpu.VMEM((32, 128, 16), jnp.float32),
             pltpu.VMEM((1, 128), jnp.float32), pltpu.VMEM((15, 1, 128), jnp.float32),
             pltpu.VMEM((1, 128), jnp.float32), pltpu.VMEM((8, 1, 128), jnp.float32),
-            dma((8 * NCH,)), dma((8 * NCH,)), dma((15,)), dma((15,)), dma((7,)), dma((7,)), dma((7,)), dma((7,)), dma,
+            dma((8 * NCH,)), dma((8 * NCH,)), dma((15,)), dma((15,)), dma((7,)), dma((7,)), dma((3,)), dma((3,)), dma,
         ],
         compiler_params=pltpu.CompilerParams(collective_id=0, has_side_effects=True),
         name="forces",

time: 54.6 us -> 54.4 us (level)
  no operation moved by 1% of the time
where the time goes in v2:
time: 54.4 us; the launch traced here: 54.2 us
  Pallas kernels  52.1 us (96%)
  local copies, waits for them, and re-layouts  1.42 us (3%)
  between operations  0.66 us (1%)
    pallas_call x1, Pallas kernels, forces(): pl.pallas_call(force_kernel, out_shape=jax.ShapeDtypeStruct((3, 32, 128),...  52.1 us
    unnamed x1, local copies, waits for them, and re-layouts  1.42 us

profile of v2, /device:TPU:1, one launch (start us, length us, event | category | flops | bytes accessed | tf_op | source)
XLA Modules:
  0.0 54.2 jit_solution(17872365638639793941)
XLA Ops:
  0.7 52.1 %forces.1 = f32[3,32,128]{2,1,0:T(8,128)} custom-call(s32[16,32]{1,0:T(8,128)} %bitcast.10, s32[1,1]{1,0:T(1,128)S(6)} %copy.6.count_ref, s32[1,64]{1,0:T(1,128)} %bitcast.11, f32[256,128]{1,0:T(8,128)} %bitcast.9), custom_call_target="tpu_custom_call" | custom-call | tf_op jit(solution)/shard_map/forces/pallas_call | solution.py:304
  52.8 1.4 %copy.7 = f32[1,1,32,3,128]{4,2,3,1,0:T(8,128)} copy(f32[1,1,32,3,128]{4,2,3,1,0:T(8,128)} %bitcast.8) | data formatting | bytes 98304
